TPU v7x, 256 devices: a whole 4x4x8 slice. The times are simulated.
256 devices in a mesh: leaf: 64 (over z, x, core), level: 4 (over y).
Axes of the slice: x: 4, y: 4, z: 8, core: 2. Of those that a mesh axis runs over, the one named last changes fastest.
Arguments:
- charges: bfloat16 [3072, 128, 256], P(('leaf', 'level')), may hold values from -6 to 6
- near_mat: bfloat16 [3072, 16, 128, 128], P(('leaf', 'level')), may hold values from -0.1875 to 0.1875
- near_source: int32 [3072, 16], P(('leaf', 'level')), may hold values from 0 to 143
- near_count: int32 [3072], P(('leaf', 'level')), may hold values from 1 to 16, as said below
- moment_map: bfloat16 [3072, 256, 128], P(('leaf', 'level')), may hold values from -0.078125 to 0.078125
- local_eval: bfloat16 [3072, 128, 256], P(('leaf', 'level')), may hold values from -0.375 to 0.375
- upward_child_translation: bfloat16 [8, 256, 256], replicated, may hold values from -0.125 to 0.125
- shift_down: bfloat16 [8, 256, 256], replicated, may hold values from -0.375 to 0.375
- transfer_ops: bfloat16 [8, 256, 256], replicated, may hold values from -0.0625 to 0.0625
- subtree_interaction_list: int32 [64, 32], P('leaf'), may hold values from 0 to 63
- subtree_interaction_operators: int32 [64, 32], P('leaf'), may hold values from 0 to 7
- parent_list: int32 [64, 8], P('leaf'), may hold values from 0 to 7
- parent_ops: int32 [64, 8], P('leaf'), may hold values from 0 to 7
Outputs:
- potential: float32 [3072, 128, 256], P(('leaf', 'level'))
Inputs may be any that keep to these rules, and one draw needn't show every extreme that they name: `near_count`: some block uses all 16 slots and some block only one.
All inputs are finite; a program needn't handle non-finite values.
Results may differ from a plain program's by a relative error of at most 0.012.
Values may be sent and summed in bfloat16 or wider, within the bound.
No kernel may reach another device: no remote copies, remote signals or barrier semaphores. Data moves between devices by JAX's collectives and lax.ppermute only.
A program may use at most 128 MiB of HBM per device.

v0:
```python
import jax
import jax.numpy as jnp
from jax import lax
from jax.sharding import PartitionSpec as P


def extended_2(cells, sides, width):
    for axis, dim in sides:
        count = lax.axis_size(axis)
        ends = count - 1
        head = lax.slice_in_dim(cells, 0, width, axis=dim)
        tail = lax.slice_in_dim(cells, cells.shape[dim] - width, cells.shape[dim], axis=dim)
        cells = jnp.concatenate(
            [
                lax.ppermute(tail, axis, [(i, (i + 1) % count) for i in range(ends)]),
                cells,
                lax.ppermute(head, axis, [((i + 1) % count, i) for i in range(ends)]),
            ],
            axis=dim,
        )
    return cells


def top_tree(
    every,
    upward_child_translation,
    shift_down,
    transfer_ops,
    subtree_interaction_list,
    subtree_interaction_operators,
    parent_list,
    parent_ops,
    leaf_index,
):
    leaves, coeffs, columns = every.shape
    grouped_terms = every.reshape(leaves // 8, 8, coeffs, columns)
    upper_levels = jnp.einsum(
        "get,kgtv->kev", upward_child_translation, grouped_terms, preferred_element_type=jnp.float32
    ).astype(jnp.bfloat16)
    coarse = jnp.einsum(
        "kcd,kdr->cr",
        transfer_ops[parent_ops[0]],
        upper_levels[parent_list[0]],
        preferred_element_type=jnp.float32,
    ).astype(jnp.bfloat16)
    far_leaf = jnp.einsum(
        "kcd,kdr->cr",
        transfer_ops[subtree_interaction_operators[0]],
        every[subtree_interaction_list[0]],
        preferred_element_type=jnp.float32,
    )
    downward = jnp.dot(shift_down[leaf_index % 8], coarse, preferred_element_type=jnp.float32)
    return (far_leaf + downward).astype(jnp.bfloat16)


def on_device(
    charges,
    near_mat,
    near_source,
    near_count,
    moment_map,
    local_eval,
    upward_child_translation,
    shift_down,
    transfer_ops,
    subtree_interaction_list,
    subtree_interaction_operators,
    parent_list,
    parent_ops,
):
    slots = near_mat.shape[1]
    subtree = lax.all_gather(charges, "level", axis=0, tiled=True)
    extended = extended_2(subtree, (("leaf", 0),), subtree.shape[0])
    picked = extended[near_source]
    active = (jnp.arange(slots, dtype=jnp.int32)[None, :] < near_count[:, None]).astype(
        jnp.bfloat16
    )
    picked = picked * active[:, :, None, None]
    near_part = jnp.einsum("bkpq,bkqr->bpr", near_mat, picked, preferred_element_type=jnp.float32)
    partial_moment = jnp.einsum(
        "bcp,bpr->cr", moment_map, charges, preferred_element_type=jnp.float32
    )
    leaf_index = lax.axis_index("leaf")
    moment = lax.psum(partial_moment.astype(jnp.bfloat16), "level")
    every = lax.all_gather(moment[None], "leaf", axis=0, tiled=True)
    local_part = top_tree(
        every,
        upward_child_translation,
        shift_down,
        transfer_ops,
        subtree_interaction_list,
        subtree_interaction_operators,
        parent_list,
        parent_ops,
        leaf_index,
    )
    far_part = jnp.einsum("bpc,cr->bpr", local_eval, local_part, preferred_element_type=jnp.float32)
    return near_part + far_part


def solution(mesh):
    placed = (
        P(("leaf", "level"), None, None),
        P(("leaf", "level"), None, None, None),
        P(("leaf", "level"), None),
        P(("leaf", "level")),
        P(("leaf", "level"), None, None),
        P(("leaf", "level"), None, None),
        P(),
        P(),
        P(),
        P("leaf", None),
        P("leaf", None),
        P("leaf", None),
        P("leaf", None),
    )
    return jax.shard_map(
        on_device,
        mesh=mesh,
        in_specs=placed,
        out_specs=P(("leaf", "level"), None, None),
        check_vma=False,
    )
```

profile of v0, /device:TPU:103, one launch (start us, length us, event | category | flops | bytes accessed | tf_op | source)
XLA Modules:
  0.0 231.8 jit_solution(3247410838116859868)
XLA Ops:
  6.5 2.5 %fusion.10 = bf16[1,256,256]{2,1,0:T(8,128)(2,1)} fusion(bf16[12,256,128]{2,1,0:T(8,128)(2,1)} %param.17, bf16[12,128,256]{2,1,0:T(8,128)(2,1)} %param.13), kind=kOutput, calls=%fused_computation.20 | convolution fusion | flops 201392128 | bytes 1703936 | tf_op jit(solution)/shard_map/bcp,bpr->cr/dot_general | solution.py:80
  9.1 0.7 all-gather.3.cloned.1.call-update
  9.8 46.2 %all-reduce.2.cloned.1.call-done = bf16[1,256,256]{2,1,0:T(8,128)(2,1)} async-done(((bf16[1,256,256]{2,1,0:T(8,128)(2,1)}), bf16[1,256,256]{2,1,0:T(8,128)(2,1)}) %all-reduce.2.cloned.1.call-update) | async-done | bytes 131088 | tf_op jit(solution)/shard_map/psum | solution.py:84
  56.0 46.2 %all-gather.3.cloned.1.call-done = bf16[48,128,256]{2,1,0:T(8,128)(2,1)} async-done(((bf16[12,128,256]{2,1,0:T(8,128)(2,1)}), bf16[48,128,256]{2,1,0:T(8,128)(2,1)}) %all-gather.3.cloned.1.call-update) | async-done | bytes 3145744 | tf_op jit(solution)/shard_map/all_gather | solution.py:72
  102.2 5.1 %collective-permute-start = (bf16[48,128,256]{2,1,0:T(8,128)(2,1)}, bf16[48,128,256]{2,1,0:T(8,128)(2,1)}, u32[]{:S(2)}, u32[]{:S(2)}) collective-permute-start(bf16[48,128,256]{2,1,0:T(8,128)(2,1)} %all-gather.3.cloned.1.call-done), channel_id=1, source_target_pairs={{0,4},{4,8},{8,12},{12,16},{16,20},{20,24},{24,28},{28,32},{32,36}... | collective-permute-start | bytes 9437192 | tf_op jit(solution)/shard_map/ppermute | solution.py:15
  107.3 1.9 collective-permute-start.1
  109.3 0.7 fusion.15
  110.0 2.9 %gather_fusion.1 = bf16[32,256,256]{2,1,0:T(8,128)(2,1)} fusion(bf16[8,256,256]{2,1,0:T(8,128)(2,1)S(1)} %copy-done, s32[1024]{0:T(1024)S(1)} %pad_clamp_fusion.3), kind=kCustom, calls=%fused_computation.1 | custom fusion | bytes 8388736 | tf_op jit(solution)/shard_map/gather | solution.py:48
  112.9 0.6 gather_fusion.3
  113.6 0.1 reshape.140
  113.8 33.0 %collective-permute-done = bf16[48,128,256]{2,1,0:T(8,128)(2,1)} collective-permute-done((bf16[48,128,256]{2,1,0:T(8,128)(2,1)}, bf16[48,128,256]{2,1,0:T(8,128)(2,1)}, u32[]{:S(2)}, u32[]{:S(2)}) %collective-permute-start) | collective-permute-done | bytes 3145760 | tf_op jit(solution)/shard_map/ppermute | solution.py:15
  146.8 7.7 %collective-permute-done.1 = bf16[48,128,256]{2,1,0:T(8,128)(2,1)} collective-permute-done((bf16[48,128,256]{2,1,0:T(8,128)(2,1)}, bf16[48,128,256]{2,1,0:T(8,128)(2,1)}, u32[]{:S(2)}, u32[]{:S(2)}) %collective-permute-start.1) | collective-permute-done | bytes 3145760 | tf_op jit(solution)/shard_map/ppermute | solution.py:17
  154.5 8.4 %pad_maximum_fusion = bf16[144,128,256]{2,1,0:T(8,128)(2,1)} fusion(bf16[48,128,256]{2,1,0:T(8,128)(2,1)} %collective-permute-done.1, bf16[48,128,256]{2,1,0:T(8,128)(2,1)} %all-gather.3.cloned.1.call-done, bf16[48,128,256]{2,1,0:T(8,128)(2,1)} %collective-permute-done), kind=kLoop, calls=%fused_computation.7 | loop fusion | flops 9437184 | bytes 18874368 | tf_op jit(solution)/shard_map/concatenate | solution.py:13
  162.9 12.0 %gather_fusion = bf16[192,128,256]{2,1,0:T(8,128)(2,1)} fusion(bf16[144,128,256]{2,1,0:T(8,128)(2,1)} %pad_maximum_fusion, s32[1024]{0:T(1024)S(1)} %pad_clamp_fusion.4), kind=kCustom, calls=%fused_computation | custom fusion | bytes 25166592 | tf_op jit(solution)/shard_map/gather | solution.py:74
  174.9 16.8 %copy.16 = bf16[12,16,128,256]{2,3,1,0:T(8,128)(2,1)} copy(bf16[12,16,128,256]{3,2,1,0:T(8,128)(2,1)} %bitcast.66) | data formatting | bytes 25165824 | tf_op jit(solution)/shard_map/gather | solution.py:74
  191.6 6.1 %gather_fusion.2 = bf16[32,256,256]{2,1,0:T(8,128)(2,1)} fusion(bf16[64,256,256]{2,1,0:T(8,128)(2,1)} %all-gather.5.cloned.1.call-done, s32[1024]{0:T(1024)S(1)} %pad_clamp_fusion.2), kind=kCustom, calls=%fused_computation.2 | custom fusion | bytes 8388736 | tf_op jit(solution)/shard_map/gather | solution.py:49
  197.8 5.3 %convolution_bitcast_fusion.1 = f32[256,256]{0,1:T(8,128)S(1)} fusion(bf16[32,256,256]{2,1,0:T(8,128)(2,1)} %gather_fusion.1, bf16[32,256,256]{2,1,0:T(8,128)(2,1)} %gather_fusion.2), kind=kOutput, calls=%fused_computation.14 | convolution fusion | flops 1073741824 | bytes 8650752 | tf_op jit(solution)/shard_map/kcd,kdr->cr/dot_general | solution.py:46
  203.1 0.5 copy-done.2
  203.6 3.7 %fusion.5 = bf16[8,256,256]{1,2,0:T(8,128)(2,1)S(1)} fusion(bf16[8,8,256,256]{3,2,1,0:T(8,128)(2,1)S(1)} %bitcast.67, bf16[8,256,256]{2,1,0:T(8,128)(2,1)} %param.19), kind=kOutput, calls=%fused_computation.11 | convolution fusion | flops 2148007936 | bytes 10485760 | tf_op jit(solution)/shard_map/get,kgtv->kev/dot_general | solution.py:37
  207.3 0.6 gather_fusion.4
  207.9 1.7 fusion.9
  209.6 1.5 fusion.20
  211.2 11.1 %bitcast_add_fusion = f32[12,128,256]{1,2,0:T(8,128)} fusion(f32[256,12,128]{2,0,1:T(8,128)S(1)} %fusion.20, bf16[12,16,128,128]{3,2,1,0:T(8,128)(2,1)} %param.14, bf16[12,16,128,256]{2,3,1,0:T(8,128)(2,1)} %copy.16, bf16[12,16]{1,0:T(8,128)(2,1)S(1)} %fusion.14), kind=kOutput, calls=%fused_computation.10 | convolution fusion | flops 1617297408 | bytes 22020480 | tf_op jit(solution)/shard_map/bkpq,bkqr->bpr/dot_general | solution.py:79
  222.3 3.0 %copy.17 = f32[12,128,256]{2,1,0:T(8,128)} copy(f32[12,128,256]{1,2,0:T(8,128)} %bitcast_add_fusion) | data formatting | bytes 3145728 | tf_op jit(solution)/shard_map/add | solution.py:98
  (31 shorter events, 0.3 us)
Async XLA Ops:
  6.5 103.4 %copy-start = (bf16[8,256,256]{2,1,0:T(8,128)(2,1)S(1)}, bf16[8,256,256]{2,1,0:T(8,128)(2,1)}, u32[]{:S(2)}) copy-start(bf16[8,256,256]{2,1,0:T(8,128)(2,1)} %param.21) | copy-start | bytes 3145732
  6.5 49.5 %all-reduce.2.cloned.1.call-start = ((), (), s32[]{:S(2)}) async-start(), calls=%async_computation.1 | async-start | bytes 262144 | tf_op jit(solution)/shard_map/psum | solution.py:84
  9.1 93.2 %all-gather.3.cloned.1.call-start = ((), (), s32[]{:S(2)}) async-start(), calls=%async_computation | async-start | bytes 3932160 | tf_op jit(solution)/shard_map/all_gather | solution.py:72
  9.8 181.8 %all-gather.5.cloned.1.call-start = ((), (), s32[]{:S(2)}) async-start(), calls=%async_computation.2 | async-start | bytes 8519680 | tf_op jit(solution)/shard_map/all_gather | solution.py:85
  102.2 44.5 %collective-permute-start = (bf16[48,128,256]{2,1,0:T(8,128)(2,1)}, bf16[48,128,256]{2,1,0:T(8,128)(2,1)}, u32[]{:S(2)}, u32[]{:S(2)}) collective-permute-start(bf16[48,128,256]{2,1,0:T(8,128)(2,1)} %all-gather.3.cloned.1.call-done), channel_id=1, source_target_pairs={{0,4},{4,8},{8,12},{12,16},{16,20},{20,24},{24,28},{28,32},{32,36}... | collective-permute-start | bytes 9437192 | tf_op jit(solution)/shard_map/ppermute | solution.py:15
  107.3 47.1 %collective-permute-start.1 = (bf16[48,128,256]{2,1,0:T(8,128)(2,1)}, bf16[48,128,256]{2,1,0:T(8,128)(2,1)}, u32[]{:S(2)}, u32[]{:S(2)}) collective-permute-start(bf16[48,128,256]{2,1,0:T(8,128)(2,1)} %all-gather.3.cloned.1.call-done), channel_id=1, source_target_pairs={{4,0},{8,4},{12,8},{16,12},{20,16},{24,20},{28,24},{32,28},{36,32}... | collective-permute-start | bytes 9437192 | tf_op jit(solution)/shard_map/ppermute | solution.py:17
  110.0 2.9 %copy-start.5 = (s32[1,8]{1,0:T(1,128)S(1)}, s32[1,8]{1,0:T(1,128)}, u32[]{:S(2)}) copy-start(s32[1,8]{1,0:T(1,128)} %param.25) | copy-start | bytes 100
  110.0 3.6 %copy-start.3 = (s32[12,16]{1,0:T(8,128)S(1)}, s32[12,16]{1,0:T(8,128)}, u32[]{:S(2)}) copy-start(s32[12,16]{1,0:T(8,128)} %param.15) | copy-start | bytes 2308
  110.0 3.6 %copy-start.6 = (s32[1,32]{1,0:T(1,128)S(1)}, s32[1,32]{1,0:T(1,128)}, u32[]{:S(2)}) copy-start(s32[1,32]{1,0:T(1,128)} %param.22) | copy-start | bytes 388
  110.0 3.7 %copy-start.7 = (s32[1,8]{1,0:T(1,128)S(1)}, s32[1,8]{1,0:T(1,128)}, u32[]{:S(2)}) copy-start(s32[1,8]{1,0:T(1,128)} %param.24) | copy-start | bytes 100
  110.0 3.7 %copy-start.4 = (s32[12]{0:T(128)S(1)}, s32[12]{0:T(128)}, u32[]{:S(2)}) copy-start(s32[12]{0:T(128)} %param.16) | copy-start | bytes 148
  197.8 5.8 %copy-start.2 = (bf16[64,256,256]{2,1,0:T(8,128)(2,1)S(1)}, bf16[64,256,256]{2,1,0:T(8,128)(2,1)}, u32[]{:S(2)}) copy-start(bf16[64,256,256]{2,1,0:T(8,128)(2,1)} %all-gather.5.cloned.1.call-done) | copy-start | bytes 25165828
  211.1 14.2 %copy-start.1 = (bf16[8,256,256]{2,1,0:T(8,128)(2,1)S(1)}, bf16[8,256,256]{2,1,0:T(8,128)(2,1)}, u32[]{:S(2)}) copy-start(bf16[8,256,256]{2,1,0:T(8,128)(2,1)} %param.21) | copy-start | bytes 3145732
Sparse Core Ops, SparseCore 0:
  9.6 46.3 all-reduce.1
  57.8 44.3 all-gather.2
  105.0 81.0 all-gather.4
where the time goes:
time: 233 us; the launch traced here: 232 us
  waiting for transfers between devices  134 us (58%)
  local copies, waits for them, and re-layouts  42.6 us (18%)
  matrix products  25.9 us (11%)
  between operations  13.3 us (6%)
  other arithmetic  9.2 us (4%)
  starting transfers between devices  7.09 us (3%)
    all_gather x1, waiting for transfers between devices, on_device(): subtree = lax.all_gather(charges, 'level', axis=0, tiled=True)  46.2 us
    psum x1, waiting for transfers between devices, on_device(): moment = lax.psum(partial_moment.astype(jnp.bfloat16), 'level')  46.2 us
    ppermute x1, waiting for transfers between devices, extended_2(): lax.ppermute(tail, axis, [(i, (i + 1) % count) for i in range(ends)])  33 us
    gather x2, local copies, waits for them, and re-layouts, on_device(): picked = extended[near_source]  28.7 us
    dot_general x1, matrix products, on_device(): jnp.einsum('bkpq,bkqr->bpr', near_mat, picked, preferred_element_type=jnp...  11.1 us
    concatenate x1, other arithmetic, extended_2(): jnp.concatenate([lax.ppermute(tail, axis, [(i, (i + 1) % count) for i in...  8.42 us
    ppermute x1, waiting for transfers between devices, extended_2(): lax.ppermute(head, axis, [((i + 1) % count, i) for i in range(ends)])  7.72 us
    gather x1, local copies, waits for them, and re-layouts, top_tree(): every[subtree_interaction_list[0]]  6.13 us
  transfers between devices with their start and end apart: 5, of which 4 were waited for; matrix products, arithmetic and copies ran while one was open for 18% of the time, Pallas kernels for 0%

commit v1 on v0

--- a/solution.py
+++ b/solution.py
@@ -81,7 +81,7 @@
         "bcp,bpr->cr", moment_map, charges, preferred_element_type=jnp.float32
     )
     leaf_index = lax.axis_index("leaf")
-    moment = lax.psum(partial_moment.astype(jnp.bfloat16), "level")
+    moment = jnp.sum(lax.all_gather(partial_moment.astype(jnp.bfloat16), "level"), axis=0)
     every = lax.all_gather(moment[None], "leaf", axis=0, tiled=True)
     local_part = top_tree(
         every,

time: 233 us -> 184 us (0.79)
  waiting for transfers between devices: 134 us -> 72.7 us
  blocking collectives: 0 us -> 11.8 us
    psum x1 -> x0, waiting for transfers between devices: 46.2 us -> none  [on_device(): moment = lax.psum(partial_moment.astype(jnp.bfloat16), 'level')]
    all_gather x1, waiting for transfers between devices: 46.2 us -> 31.3 us  [on_device(): subtree = lax.all_gather(charges, 'level', axis=0, tiled=True)]
    all_gather x0 -> x1, blocking collectives: none -> 11.8 us  [on_device(): lax.all_gather(partial_moment.astype(jnp.bfloat16), 'level')]
  transfers between devices with their start and end apart: 5 -> 4, of which waited for: 4 -> 3; matrix products, arithmetic and copies ran while one was open for 18% -> 24% of each run, Pallas kernels for 0% -> 0%
where the time goes in v1:
time: 184 us; the launch traced here: 183 us
  waiting for transfers between devices  72.7 us (40%)
  local copies, waits for them, and re-layouts  42.5 us (23%)
  matrix products  25.1 us (14%)
  between operations  13.6 us (7%)
  blocking collectives  11.8 us (6%)
  other arithmetic  9.94 us (5%)
  starting transfers between devices  7.05 us (4%)
    ppermute x1, waiting for transfers between devices, extended_2(): lax.ppermute(tail, axis, [(i, (i + 1) % count) for i in range(ends)])  33 us
    all_gather x1, waiting for transfers between devices, on_device(): subtree = lax.all_gather(charges, 'level', axis=0, tiled=True)  31.3 us
    gather x2, local copies, waits for them, and re-layouts, on_device(): picked = extended[near_source]  28.7 us
    all_gather x1, blocking collectives, on_device(): lax.all_gather(partial_moment.astype(jnp.bfloat16), 'level')  11.8 us
    dot_general x1, matrix products, on_device(): jnp.einsum('bkpq,bkqr->bpr', near_mat, picked, preferred_element_type=jnp...  11.1 us
    concatenate x1, other arithmetic, extended_2(): jnp.concatenate([lax.ppermute(tail, axis, [(i, (i + 1) % count) for i in...  8.41 us
    ppermute x1, waiting for transfers between devices, extended_2(): lax.ppermute(head, axis, [((i + 1) % count, i) for i in range(ends)])  7.72 us
    gather x1, local copies, waits for them, and re-layouts, top_tree(): every[subtree_interaction_list[0]]  6.12 us
  transfers between devices with their start and end apart: 4, of which 3 were waited for; matrix products, arithmetic and copies ran while one was open for 24% of the time, Pallas kernels for 0%

profile of v1, /device:TPU:103, one launch (start us, length us, event | category | flops | bytes accessed | tf_op | source)
XLA Modules:
  0.0 182.7 jit_solution(17348469819178732740)
XLA Ops:
  6.5 0.7 all-gather.5.cloned.1.call-update
  7.3 1.7 fusion.7
  9.0 11.8 %all-gather = bf16[1024,256]{1,0:T(8,128)(2,1)S(1)} all-gather(bf16[256,256]{1,0:T(8,128)(2,1)S(1)} %fusion.7), channel_id=2, replica_groups=mesh['leaf'=64,'level'=4] {'level'}, dimensions={0}, use_global_device_ids=true | all-gather | bytes 655360 | tf_op jit(solution)/shard_map/all_gather | solution.py:84
  20.8 0.7 reduce_sum.12
  21.6 31.3 %all-gather.5.cloned.1.call-done = bf16[48,128,256]{2,1,0:T(8,128)(2,1)} async-done(((bf16[12,128,256]{2,1,0:T(8,128)(2,1)}), bf16[48,128,256]{2,1,0:T(8,128)(2,1)}) %all-gather.5.cloned.1.call-update) | async-done | bytes 3145744 | tf_op jit(solution)/shard_map/all_gather | solution.py:72
  52.9 5.1 %collective-permute-start = (bf16[48,128,256]{2,1,0:T(8,128)(2,1)}, bf16[48,128,256]{2,1,0:T(8,128)(2,1)}, u32[]{:S(2)}, u32[]{:S(2)}) collective-permute-start(bf16[48,128,256]{2,1,0:T(8,128)(2,1)} %all-gather.5.cloned.1.call-done), channel_id=1, source_target_pairs={{0,4},{4,8},{8,12},{12,16},{16,20},{20,24},{24,28},{28,32},{32,36}... | collective-permute-start | bytes 9437192 | tf_op jit(solution)/shard_map/ppermute | solution.py:15
  58.0 1.9 %collective-permute-start.1 = (bf16[48,128,256]{2,1,0:T(8,128)(2,1)}, bf16[48,128,256]{2,1,0:T(8,128)(2,1)}, u32[]{:S(2)}, u32[]{:S(2)}) collective-permute-start(bf16[48,128,256]{2,1,0:T(8,128)(2,1)} %all-gather.5.cloned.1.call-done), channel_id=1, source_target_pairs={{4,0},{8,4},{12,8},{16,12},{20,16},{24,20},{28,24},{32,28},{36,32}... | collective-permute-start | bytes 9437192 | tf_op jit(solution)/shard_map/ppermute | solution.py:17
  59.9 0.7 fusion.14
  60.7 2.9 %gather_fusion.1 = bf16[32,256,256]{2,1,0:T(8,128)(2,1)} fusion(bf16[8,256,256]{2,1,0:T(8,128)(2,1)S(1)} %copy-done, s32[1024]{0:T(1024)S(1)} %pad_clamp_fusion.3), kind=kCustom, calls=%fused_computation.1 | custom fusion | bytes 8388736 | tf_op jit(solution)/shard_map/gather | solution.py:48
  63.6 0.6 gather_fusion.3
  64.4 33.0 %collective-permute-done = bf16[48,128,256]{2,1,0:T(8,128)(2,1)} collective-permute-done((bf16[48,128,256]{2,1,0:T(8,128)(2,1)}, bf16[48,128,256]{2,1,0:T(8,128)(2,1)}, u32[]{:S(2)}, u32[]{:S(2)}) %collective-permute-start) | collective-permute-done | bytes 3145760 | tf_op jit(solution)/shard_map/ppermute | solution.py:15
  97.4 7.7 %collective-permute-done.1 = bf16[48,128,256]{2,1,0:T(8,128)(2,1)} collective-permute-done((bf16[48,128,256]{2,1,0:T(8,128)(2,1)}, bf16[48,128,256]{2,1,0:T(8,128)(2,1)}, u32[]{:S(2)}, u32[]{:S(2)}) %collective-permute-start.1) | collective-permute-done | bytes 3145760 | tf_op jit(solution)/shard_map/ppermute | solution.py:17
  105.1 8.4 %pad_maximum_fusion = bf16[144,128,256]{2,1,0:T(8,128)(2,1)} fusion(bf16[48,128,256]{2,1,0:T(8,128)(2,1)} %collective-permute-done.1, bf16[48,128,256]{2,1,0:T(8,128)(2,1)} %all-gather.5.cloned.1.call-done, bf16[48,128,256]{2,1,0:T(8,128)(2,1)} %collective-permute-done), kind=kLoop, calls=%fused_computation.7 | loop fusion | flops 9437184 | bytes 18874368 | tf_op jit(solution)/shard_map/concatenate | solution.py:13
  113.5 11.9 %gather_fusion = bf16[192,128,256]{2,1,0:T(8,128)(2,1)} fusion(bf16[144,128,256]{2,1,0:T(8,128)(2,1)} %pad_maximum_fusion, s32[1024]{0:T(1024)S(1)} %pad_clamp_fusion.4), kind=kCustom, calls=%fused_computation | custom fusion | bytes 25166592 | tf_op jit(solution)/shard_map/gather | solution.py:74
  125.5 16.7 %copy.16 = bf16[12,16,128,256]{2,3,1,0:T(8,128)(2,1)} copy(bf16[12,16,128,256]{3,2,1,0:T(8,128)(2,1)} %bitcast.64) | data formatting | bytes 25165824 | tf_op jit(solution)/shard_map/gather | solution.py:74
  142.2 6.1 %gather_fusion.2 = bf16[32,256,256]{2,1,0:T(8,128)(2,1)} fusion(bf16[64,256,256]{2,1,0:T(8,128)(2,1)} %bitcast.66, s32[1024]{0:T(1024)S(1)} %pad_clamp_fusion.2), kind=kCustom, calls=%fused_computation.2 | custom fusion | bytes 8388736 | tf_op jit(solution)/shard_map/gather | solution.py:49
  148.3 5.3 %convolution_bitcast_fusion.1 = f32[256,256]{0,1:T(8,128)S(1)} fusion(bf16[32,256,256]{2,1,0:T(8,128)(2,1)} %gather_fusion.1, bf16[32,256,256]{2,1,0:T(8,128)(2,1)} %gather_fusion.2), kind=kOutput, calls=%fused_computation.14 | convolution fusion | flops 1073741824 | bytes 8650752 | tf_op jit(solution)/shard_map/kcd,kdr->cr/dot_general | solution.py:46
  153.7 0.5 copy-done.2
  154.2 3.7 %fusion.5 = bf16[8,256,256]{1,2,0:T(8,128)(2,1)S(1)} fusion(bf16[8,8,256,256]{3,2,1,0:T(8,128)(2,1)S(1)} %bitcast.67, bf16[8,256,256]{2,1,0:T(8,128)(2,1)} %param.19), kind=kOutput, calls=%fused_computation.11 | convolution fusion | flops 2148007936 | bytes 10485760 | tf_op jit(solution)/shard_map/get,kgtv->kev/dot_general | solution.py:37
  157.9 0.6 gather_fusion.4
  158.5 1.7 fusion.9
  160.2 1.5 fusion.19
  161.7 11.1 %bitcast_add_fusion = f32[12,128,256]{1,2,0:T(8,128)} fusion(f32[256,12,128]{2,0,1:T(8,128)S(1)} %fusion.19, bf16[12,16,128,128]{3,2,1,0:T(8,128)(2,1)} %param.14, bf16[12,16,128,256]{2,3,1,0:T(8,128)(2,1)} %copy.16, bf16[12,16]{1,0:T(8,128)(2,1)S(1)} %fusion.13), kind=kOutput, calls=%fused_computation.10 | convolution fusion | flops 1617297408 | bytes 22020480 | tf_op jit(solution)/shard_map/bkpq,bkqr->bpr/dot_general | solution.py:79
  172.9 3.0 %copy.17 = f32[12,128,256]{2,1,0:T(8,128)} copy(f32[12,128,256]{1,2,0:T(8,128)} %bitcast_add_fusion) | data formatting | bytes 3145728 | tf_op jit(solution)/shard_map/add | solution.py:98
  (30 shorter events, 0.3 us)
Async XLA Ops:
  6.5 54.1 %copy-start = (bf16[8,256,256]{2,1,0:T(8,128)(2,1)S(1)}, bf16[8,256,256]{2,1,0:T(8,128)(2,1)}, u32[]{:S(2)}) copy-start(bf16[8,256,256]{2,1,0:T(8,128)(2,1)} %param.21) | copy-start | bytes 3145732
  6.5 46.3 %all-gather.5.cloned.1.call-start = ((), (), s32[]{:S(2)}) async-start(), calls=%async_computation | async-start | bytes 3932160 | tf_op jit(solution)/shard_map/all_gather | solution.py:72
  7.3 135.0 %all-gather.7.cloned.1.call-start = ((), (), s32[]{:S(2)}) async-start(), calls=%async_computation.1 | async-start | bytes 8519680 | tf_op jit(solution)/shard_map/all_gather | solution.py:85
  52.9 44.5 %collective-permute-start = (bf16[48,128,256]{2,1,0:T(8,128)(2,1)}, bf16[48,128,256]{2,1,0:T(8,128)(2,1)}, u32[]{:S(2)}, u32[]{:S(2)}) collective-permute-start(bf16[48,128,256]{2,1,0:T(8,128)(2,1)} %all-gather.5.cloned.1.call-done), channel_id=1, source_target_pairs={{0,4},{4,8},{8,12},{12,16},{16,20},{20,24},{24,28},{28,32},{32,36}... | collective-permute-start | bytes 9437192 | tf_op jit(solution)/shard_map/ppermute | solution.py:15
  58.0 47.1 %collective-permute-start.1 = (bf16[48,128,256]{2,1,0:T(8,128)(2,1)}, bf16[48,128,256]{2,1,0:T(8,128)(2,1)}, u32[]{:S(2)}, u32[]{:S(2)}) collective-permute-start(bf16[48,128,256]{2,1,0:T(8,128)(2,1)} %all-gather.5.cloned.1.call-done), channel_id=1, source_target_pairs={{4,0},{8,4},{12,8},{16,12},{20,16},{24,20},{28,24},{32,28},{36,32}... | collective-permute-start | bytes 9437192 | tf_op jit(solution)/shard_map/ppermute | solution.py:17
  60.6 2.9 %copy-start.5 = (s32[1,8]{1,0:T(1,128)S(1)}, s32[1,8]{1,0:T(1,128)}, u32[]{:S(2)}) copy-start(s32[1,8]{1,0:T(1,128)} %param.25) | copy-start | bytes 100
  60.6 3.6 %copy-start.3 = (s32[12,16]{1,0:T(8,128)S(1)}, s32[12,16]{1,0:T(8,128)}, u32[]{:S(2)}) copy-start(s32[12,16]{1,0:T(8,128)} %param.15) | copy-start | bytes 2308
  60.6 3.7 %copy-start.6 = (s32[1,32]{1,0:T(1,128)S(1)}, s32[1,32]{1,0:T(1,128)}, u32[]{:S(2)}) copy-start(s32[1,32]{1,0:T(1,128)} %param.22) | copy-start | bytes 388
  60.6 3.7 %copy-start.7 = (s32[1,8]{1,0:T(1,128)S(1)}, s32[1,8]{1,0:T(1,128)}, u32[]{:S(2)}) copy-start(s32[1,8]{1,0:T(1,128)} %param.24) | copy-start | bytes 100
  60.6 3.7 %copy-start.4 = (s32[12]{0:T(128)S(1)}, s32[12]{0:T(128)}, u32[]{:S(2)}) copy-start(s32[12]{0:T(128)} %param.16) | copy-start | bytes 148
  148.3 5.8 %copy-start.2 = (bf16[16384,256]{1,0:T(8,128)(2,1)S(1)}, bf16[16384,256]{1,0:T(8,128)(2,1)}, u32[]{:S(2)}) copy-start(bf16[16384,256]{1,0:T(8,128)(2,1)} %all-gather.7.cloned.1.call-done) | copy-start | bytes 25165828
  161.7 14.1 %copy-start.1 = (bf16[8,256,256]{2,1,0:T(8,128)(2,1)S(1)}, bf16[8,256,256]{2,1,0:T(8,128)(2,1)}, u32[]{:S(2)}) copy-start(bf16[8,256,256]{2,1,0:T(8,128)(2,1)} %param.21) | copy-start | bytes 3145732
Sparse Core Ops, SparseCore 0:
  9.1 43.6 all-gather.4
  55.6 81.0 all-gather.6
